TPU v7x, 256 devices: a whole 4x4x8 slice. The times are simulated.
256 devices in a mesh: row: 8 (over y, core), col: 32 (over z, x).
Axes of the slice: x: 4, y: 4, z: 8, core: 2. Of those that a mesh axis runs over, the one named last changes fastest.
Arguments:
- amps: bfloat16 [1024, 256, 256], P('row', 'col'), may hold values from -6 to 6
- ints: bfloat16 [16384, 256, 256], P(('row', 'col')), may hold values from -0.0234375 to 0.0234375
- task_cd: int32 [16384], P(('row', 'col')), may hold values from 0 to 7, as said below
- task_ab: int32 [16384], P(('row', 'col')), may hold values from 0 to 7
- task_count: int32 [256], P(('row', 'col')), may hold values from 8 to 64, as said below
Outputs:
- residual: bfloat16 [1024, 64, 256], P('col', 'row')
Inputs may be any that keep to these rules, and one draw needn't show every extreme that they name: On each device the slots name distinct (task_cd, task_ab) pairs. The live slots of a device are its first task_count ones; some device has all 64 slots live in every draw.
All inputs are finite; a program needn't handle non-finite values.
Results may differ from a plain program's by a relative error of at most 0.001.
Values may be sent and summed in bfloat16 or wider, within the bound.
A program may use at most 128 MiB of HBM per device.

v0:
```python
import jax
import jax.numpy as jnp
from jax import lax
from jax.sharding import Mesh
from jax.sharding import PartitionSpec as P

CD_COL = 8
PAIR_TILES_ROW = 8
COL = ("col_0", "col_1")
ROW_COL = ("row", "col_0", "col_1")


def sum_by_axis(value, axes, dim):
    for axis in axes:
        value = lax.psum_scatter(value, axis, scatter_dimension=dim, tiled=True)
    return value


def dense_tiles(ints, task_cd, task_ab, count):
    slots = ints.shape[0]
    order = jnp.arange(slots, dtype=jnp.int32)
    live = order < count
    wanted = jnp.arange(PAIR_TILES_ROW * CD_COL, dtype=jnp.int32)[:, None]
    slot_key = task_ab * CD_COL + task_cd
    match = (slot_key[None, :] == wanted) & live[None, :]
    found = jnp.sum(jnp.where(match, order[None, :], 0), axis=1)
    present_mask = jnp.any(match, axis=1)
    table = jnp.take(ints, found, axis=0) * present_mask.astype(ints.dtype)[:, None, None]
    return table.reshape(PAIR_TILES_ROW, CD_COL, ints.shape[1], ints.shape[2])


def ladder_term(rows_amps, table):
    return jnp.einsum("nkt,aktu->nau", rows_amps, table, preferred_element_type=jnp.float32)


def shards(amps, ints, task_cd, task_ab, task_count):
    whole = lax.all_gather(amps, "row", axis=0, tiled=True)
    table = dense_tiles(ints, task_cd, task_ab, task_count[0])
    partial_sum = ladder_term(whole, table)
    summed = sum_by_axis(partial_sum, COL, 0)
    return summed.astype(jnp.bfloat16)


def solution(mesh):
    finer = Mesh(mesh.devices.reshape(mesh.shape["row"], 8, 4), ("row", "col_0", "col_1"))
    in_specs = (P("row", COL, None), P(ROW_COL, None, None), P(ROW_COL), P(ROW_COL), P(ROW_COL))
    out_specs = P(COL, "row", None)
    return jax.shard_map(
        shards, mesh=finer, in_specs=in_specs, out_specs=out_specs, check_vma=False
    )
```

profile of v0, /device:TPU:16, one launch (start us, length us, event | category | flops | bytes accessed | tf_op | source)
XLA Modules:
  0.0 192.0 jit_solution(13895775385929147668)
XLA Ops:
  6.5 0.0 all-gather.2.cloned.1.call-start
  6.5 1.9 %copy.13 = bf16[128,8,256]{2,0,1:T(8,128)(2,1)} copy(bf16[128,8,256]{2,1,0:T(8,128)(2,1)} %param.5) | data formatting | bytes 1048576 | tf_op args[0]
  8.5 0.0 all-gather.2.cloned.1.call-update
  8.5 0.0 reduce-scatter.3.cloned.1.call-start
  9.2 0.7 multiply_add_fusion
  9.9 0.1 fusion.13
  10.0 0.1 reshape.35
  10.1 0.1 select_reduce_fusion
  10.2 0.1 reduce_sum.14
  10.3 8.9 %gather_fusion = bf16[64,256,256]{2,1,0:T(8,128)(2,1)} fusion(bf16[64,256,256]{2,1,0:T(8,128)(2,1)} %param.6, s32[1024]{0:T(1024)S(1)} %pad_clamp_fusion), kind=kCustom, calls=%fused_computation | custom fusion | bytes 16777472 | tf_op jit(solution)/shard_map/jit(_take)/gather | solution.py:28
  19.2 11.6 %copy.12 = bf16[8,8,256,256]{2,3,1,0:T(8,128)(2,1)} copy(bf16[8,8,256,256]{3,2,1,0:T(8,128)(2,1)} %bitcast.17) | data formatting | bytes 16777216 | tf_op jit(solution)/shard_map/jit(_take)/gather | solution.py:28
  30.9 14.4 %all-gather.2.cloned.1.call-done = bf16[1024,8,256]{2,0,1:T(8,128)(2,1)} async-done(((bf16[128,8,256]{2,0,1:T(8,128)(2,1)}), bf16[1024,8,256]{2,0,1:T(8,128)(2,1)}) %all-gather.2.cloned.1.call-update) | async-done | bytes 4194320 | tf_op jit(solution)/shard_map/all_gather | solution.py:37
  45.3 14.5 %fusion.7 = f32[1024,8,256]{0,2,1:T(8,128)} fusion(bf16[1024,8,256]{2,0,1:T(8,128)(2,1)} %all-gather.2.cloned.1.call-done, bf16[8,8,256,256]{2,3,1,0:T(8,128)(2,1)} %copy.12, pred[8,8]{1,0:T(8,128)(4,1)S(1)} %compare_and_fusion, bf16[8,8]{1,0:T(8,128)(2,1)S(1)} %reshape.35), kind=kOutput, calls=%fused_computation.8 | convolution fusion | flops 8598323200 | bytes 20971712 | tf_op jit(solution)/shard_map/nkt,aktu->nau/dot_general | solution.py:33
  59.8 0.0 reduce-scatter.3.cloned.1.call-update
  59.8 0.0 reduce-scatter.5.cloned.1.call-start
  59.9 96.3 %reduce-scatter.3.cloned.1.call-done = f32[128,8,256]{0,2,1:T(8,128)} async-done(((f32[1024,8,256]{0,2,1:T(8,128)}), f32[128,8,256]{0,2,1:T(8,128)}) %reduce-scatter.3.cloned.1.call-update) | async-done | bytes 1048592 | tf_op jit(solution)/shard_map/reduce_scatter | solution.py:15
  156.2 2.7 %copy.14 = f32[128,8,256]{2,1,0:T(8,128)} copy(f32[128,8,256]{0,2,1:T(8,128)} %reduce-scatter.3.cloned.1.call-done) | data formatting | bytes 2097152 | tf_op jit(solution)/shard_map/reduce_scatter | solution.py:15
  158.8 0.0 reduce-scatter.5.cloned.1.call-update
  158.9 25.0 %reduce-scatter.5.cloned.1.call-done = f32[32,8,256]{2,1,0:T(8,128)} async-done(((f32[128,8,256]{2,1,0:T(8,128)}), f32[32,8,256]{2,1,0:T(8,128)}) %reduce-scatter.5.cloned.1.call-update) | async-done | bytes 262160 | tf_op jit(solution)/shard_map/reduce_scatter | solution.py:15
  183.9 1.6 convert_element_type.15
  (5 shorter events, 0.0 us)
Async XLA Ops:
  6.5 38.7 %all-gather.2.cloned.1.call-start = ((), (), s32[]{:S(2)}) async-start(), calls=%async_computation.2 | async-start | bytes 4718592 | tf_op jit(solution)/shard_map/all_gather | solution.py:37
  8.5 147.7 %reduce-scatter.3.cloned.1.call-start = ((), (), s32[]{:S(2)}) async-start(), calls=%async_computation.3 | async-start | bytes 9437184 | tf_op jit(solution)/shard_map/reduce_scatter | solution.py:15
  59.8 124.1 %reduce-scatter.5.cloned.1.call-start = ((), (), s32[]{:S(2)}) async-start(), calls=%async_computation.4 | async-start | bytes 1310720 | tf_op jit(solution)/shard_map/reduce_scatter | solution.py:15
Sparse Core Ops, SparseCore 0:
  9.2 36.0 all-gather.1
  59.9 96.2 reduce-scatter.2
  159.0 24.8 reduce-scatter.4
where the time goes:
time: 193 us; the launch traced here: 192 us
  waiting for transfers between devices  136 us (70%)
  local copies, waits for them, and re-layouts  25.3 us (13%)
  matrix products  14.5 us (8%)
  between operations  13.8 us (7%)
  other arithmetic  2.57 us (1%)
    reduce_scatter x2, waiting for transfers between devices, sum_by_axis(): value = lax.psum_scatter(value, axis, scatter_dimension=dim, tiled=True)  121 us
    gather x2, local copies, waits for them, and re-layouts, dense_tiles(): jnp.take(ints, found, axis=0)  20.5 us
    dot_general x1, matrix products, ladder_term(): jnp.einsum('nkt,aktu->nau', rows_amps, table, preferred_element_type=jnp....  14.5 us
    all_gather x1, waiting for transfers between devices, shards(): whole = lax.all_gather(amps, 'row', axis=0, tiled=True)  14.4 us
  transfers between devices with their start and end apart: 3, of which 3 were waited for; matrix products, arithmetic and copies ran while one was open for 11% of the time, Pallas kernels for 0%

commit v1 on v0

v1 whole, which is shorter than its diff:
```python
import functools

import jax
import jax.numpy as jnp
from jax import lax
from jax.experimental import pallas as pl
from jax.experimental.pallas import tpu as pltpu
from jax.sharding import PartitionSpec as P

MESH = pl.DeviceIdType.MESH
NX, NY, NZ = 4, 4, 8
TILE = 256
KT = 8
AT = 8
WIDE = AT * TILE
LANES = WIDE // 128
STEPS, GROUPS = 4, 8
TOP = 32000.0
OCTAVE = 16.0
HALF_MSG = GROUPS * LANES // 4 + 1
FULL_MSG = GROUPS * LANES // 2 + 1
ROW_MSG = LANES // 2 + 1


def place(delta, core, q):
    if delta == 0:
        return 0, core * 4 + q
    if delta == 2:
        return 2 + q // 2, 4 + core * 2 + q % 2
    d = 0 if delta == 1 else 1
    if q < 2:
        return 1, d * 4 + core * 2 + q
    return q, d * 2 + core


def group_of(step, g, y):
    if step == 0:
        return 2 * y + g // 4, g % 4
    if step == 1:
        delta, core, q = 1 + 2 * (g // 4), (g // 2) % 2, g % 2
    else:
        first = g < 4
        delta = jnp.where(first, 1 + 2 * (g // 2), 2)
        core = jnp.where(first, g % 2, (g - 4) // 2)
        q = jnp.where(first, step, 2 * (step - 2) + g % 2)
    return 2 * lax.rem(y + delta, NY) + core, q


def kernel(
    amps_ref, ints_ref, cd_ref, ab_ref, count_ref, out_ref,
    tiles, wide, table_v, table_s, lhs, part, hs, hr, fs, fr, zs, zr, own,
    ints_sem, table_sem, core_send, y_send, ag_recv,
    h_send, h_recv, f_send, f_recv, z_send, z_recv,
):
    row, col = lax.axis_index("row"), lax.axis_index("col")
    y, core = row // 2, row % 2
    z, x = col // NX, col % NX
    partner = (2 * y + 1 - core, col)
    y_up = (2 * lax.rem(y + 1, NY) + core, col)
    y_down = (2 * lax.rem(y + NY - 1, NY) + core, col)
    x_right, x_left = lax.rem(x + 1, NX), lax.rem(x + NX - 1, NX)
    right, left = (row, z * NX + x_right), (row, z * NX + x_left)
    lane = lax.broadcasted_iota(jnp.int32, (8, 128), 1)

    barrier = pltpu.get_barrier_semaphore()
    for peer in (partner, y_up, y_down, right, left):
        pl.semaphore_signal(barrier, inc=1, device_id=peer, device_id_type=MESH)
    for dz in range(1, NZ):
        peer = (row, lax.rem(z + dz, NZ) * NX + x)
        pl.semaphore_signal(barrier, inc=1, device_id=peer, device_id_type=MESH)

    load = pltpu.make_async_copy(ints_ref, tiles.at[pl.ds(0, KT * AT)], ints_sem)
    load.start()

    whole = amps_ref[...].astype(jnp.float32).reshape(128 * KT, TILE)
    for side in range(2):
        wide[side] = whole[:, side * 128 : (side + 1) * 128]
    for q in range(4):
        start = pl.multiple_of((core * 4 + q) * 32, 32)
        for k in range(KT):
            for side in range(2):
                rows = [wide[side, pl.ds((32 * xd + 8 * q) * KT + k, 8, stride=KT), :] for xd in range(NX)]
                at = k * TILE + side * 128
                lhs[0, pl.ds(start, 32), at : at + 128] = jnp.concatenate(rows, 0).astype(jnp.bfloat16)

    pl.semaphore_wait(barrier, 12)

    def block(step, g):
        return lhs.at[step, pl.ds(pl.multiple_of(g * 32, 32), 32), :]

    def send(src, dst, send_sem, recv_sem, to):
        copy = pltpu.make_async_remote_copy(
            src_ref=src, dst_ref=dst, send_sem=send_sem, recv_sem=recv_sem, device_id=to, device_id_type=MESH
        )
        copy.start()
        return copy

    def arrived(ref, sem):
        pltpu.make_async_remote_copy(
            src_ref=ref, dst_ref=ref, send_sem=core_send.at[0, 0], recv_sem=sem, device_id=partner, device_id_type=MESH
        ).wait_recv()

    pending = []
    mine = [block(0, core * 4 + q) for q in range(4)]
    for q in range(4):
        s, g = place(0, core, q)
        pending.append(send(mine[q], mine[q], core_send.at[0, q], ag_recv.at[s, g], partner))
    for q in range(4):
        s, g = place(3, core, q)
        pending.append(send(mine[q], block(s, g), y_send.at[0, q], ag_recv.at[s, g], y_up))
        s, g = place(1, core, q)
        pending.append(send(mine[q], block(s, g), y_send.at[1, q], ag_recv.at[s, g], y_down))

    def pass_on(delta, q):
        s, g = place(delta, core, q)
        arrived(block(s, g), ag_recv.at[s, g])
        pending.append(send(block(s, g), block(s, g), core_send.at[delta, q], ag_recv.at[s, g], partner))
        s2, g2 = place(2, core, q)
        if delta == 1 and q % 2 == 0:
            pending.append(send(block(s, g), block(s2, g2), y_send.at[2, q], ag_recv.at[s2, g2], y_down))
        if delta == 3 and q % 2 == 1:
            pending.append(send(block(s, g), block(s2, g2), y_send.at[2, q], ag_recv.at[s2, g2], y_up))

    def from_partner(delta, q):
        s, g = place(delta, 1 - core, q)
        arrived(block(s, g), ag_recv.at[s, g])

    count = count_ref[0]

    def note(slot, table):
        key = jnp.where(slot < count, ab_ref[slot] * KT + cd_ref[slot], -1)
        return jnp.where(lane == key, slot, table)

    table_v[...] = lax.fori_loop(0, KT * AT, note, jnp.full((8, 128), KT * AT, jnp.int32))
    tiles[KT * AT] = jnp.zeros((TILE, TILE), jnp.bfloat16)
    move = pltpu.make_async_copy(table_v, table_s, table_sem)
    move.start()
    move.wait()
    load.wait()

    def multiply(step):
        def one(a, carry):
            total = None
            for k in range(KT):
                term = jnp.dot(
                    lhs[step, :, k * TILE : (k + 1) * TILE],
                    tiles[table_s[0, a * KT + k]],
                    preferred_element_type=jnp.float32,
                )
                total = term if total is None else total + term
            part[step, :, pl.ds(pl.multiple_of(a * TILE, TILE), TILE)] = total
            return carry

        lax.fori_loop(0, AT, one, 0)

    def scale_of(code):
        return jnp.exp2(code * (1.0 / OCTAVE)) * (1.0 / TOP)

    def encode(values, store):
        top = functools.reduce(jnp.maximum, [jnp.abs(v) for v in values])
        top = jnp.maximum(jnp.max(top, axis=1, keepdims=True), 1e-30)
        code = jnp.ceil(jnp.log2(top) * OCTAVE)
        factor = 1.0 / scale_of(code)
        codes = [jnp.round(v * factor).astype(jnp.int32) for v in values]
        half = len(values) // 2
        for c in range(half):
            store(c, jnp.concatenate([codes[c], codes[c + half]], 0).astype(jnp.int16))
        return code

    def decode(words, scale):
        pairs = [w.astype(jnp.int32).astype(jnp.float32) for w in words]
        return [p[:8] * scale for p in pairs] + [p[8:] * scale for p in pairs]

    def two_rows(code):
        code = code.astype(jnp.int32)
        return jnp.concatenate([code, code], 0).astype(jnp.int16)

    def scales_in(message):
        return scale_of(message.astype(jnp.int32).astype(jnp.float32)[:8])

    def scale_at(scales, g):
        return jnp.sum(jnp.where(lane == g, scales, 0.0), axis=1, keepdims=True)

    def partial_row(step, g, xd, first, last):
        rows = pl.ds(pl.multiple_of(g * 32 + xd * 8, 8), 8)
        return [part[step, rows, c * 128 : (c + 1) * 128] for c in range(first, last)]

    half = LANES // 2

    def send_halves(step):
        across = lax.rem(x + 2, NX)
        for way, to in ((0, right), (1, left)):
            def one(g, codes, way=way):
                values = partial_row(step, g, across, way * half, (way + 1) * half)

                def store(c, word):
                    hs[step, way, g * (half // 2) + c] = word

                return jnp.where(lane == g, encode(values, store), codes)

            codes = lax.fori_loop(0, GROUPS, one, jnp.zeros((8, 128), jnp.float32))
            hs[step, way, HALF_MSG - 1] = two_rows(codes)
            pending.append(send(hs.at[step, way], hr.at[step, way], h_send.at[step, way], h_recv.at[step, way], to))

    def send_full(step):
        for way, to, xd in ((0, right, x_right), (1, left, x_left)):
            arrived(hr.at[step, way], h_recv.at[step, way])
            scales = scales_in(hr[step, way, HALF_MSG - 1])

            def one(g, codes, way=way, xd=xd, scales=scales):
                values = partial_row(step, g, xd, 0, LANES)
                words = [hr[step, way, g * (half // 2) + c] for c in range(half // 2)]
                added = decode(words, scale_at(scales, g))
                for c in range(half):
                    values[way * half + c] = values[way * half + c] + added[c]

                def store(c, word):
                    fs[step, way, g * half + c] = word

                return jnp.where(lane == g, encode(values, store), codes)

            codes = lax.fori_loop(0, GROUPS, one, jnp.zeros((8, 128), jnp.float32))
            fs[step, way, FULL_MSG - 1] = two_rows(codes)
            pending.append(send(fs.at[step, way], fr.at[step, way], f_send.at[step, way], f_recv.at[step, way], to))

    def row_copy(step, g, zd, q):
        return pltpu.make_async_remote_copy(
            src_ref=zs.at[step, g], dst_ref=zr.at[z, q], send_sem=z_send.at[step, g], recv_sem=z_recv.at[z, q],
            device_id=(row, zd * NX + x), device_id_type=MESH,
        )

    def send_rows(step):
        scales = []
        for way in range(2):
            arrived(fr.at[step, way], f_recv.at[step, way])
            scales.append(scales_in(fr[step, way, FULL_MSG - 1]))

        def one(g, carry):
            values = partial_row(step, g, x, 0, LANES)
            for way in range(2):
                words = [fr[step, way, g * half + c] for c in range(half)]
                added = decode(words, scale_at(scales[way], g))
                values = [v + w for v, w in zip(values, added)]
            zd, q = group_of(step, g, y)

            @pl.when(zd == z)
            def _():
                for c in range(LANES):
                    own[q, :, c * 128 : (c + 1) * 128] = values[c]

            @pl.when(zd != z)
            def _():
                def store(c, word):
                    zs[step, g, c] = word

                code = encode(values, store)
                zs[step, g, ROW_MSG - 1] = two_rows(jnp.broadcast_to(code, (8, 128)))
                row_copy(step, g, zd, q).start()

            return carry

        lax.fori_loop(0, GROUPS, one, 0)

    for q in range(4):
        from_partner(0, q)
    multiply(0)
    send_halves(0)

    for q in range(2):
        pass_on(1, q)
        pass_on(3, q)
    send_full(0)
    for q in range(2):
        from_partner(1, q)
        from_partner(3, q)
    multiply(1)
    send_halves(1)

    pass_on(1, 2)
    pass_on(3, 2)
    pass_on(1, 3)
    pass_on(3, 3)
    send_full(1)
    send_rows(0)
    pass_on(2, 0)
    pass_on(2, 1)
    from_partner(1, 2)
    from_partner(3, 2)
    from_partner(2, 0)
    from_partner(2, 1)
    multiply(2)
    send_halves(2)

    pass_on(2, 2)
    pass_on(2, 3)
    send_full(2)
    send_rows(1)
    from_partner(1, 3)
    from_partner(3, 3)
    from_partner(2, 2)
    from_partner(2, 3)
    multiply(3)
    send_halves(3)
    send_rows(2)
    send_full(3)
    send_rows(3)

    def gather(n, carry):
        source, q = lax.rem(z + 1 + n // 4, NZ), n % 4
        arrived(zr.at[source, q], z_recv.at[source, q])
        scale = scales_in(zr[source, q, ROW_MSG - 1])
        added = decode([zr[source, q, c] for c in range(half)], scale)
        for c in range(LANES):
            own[q, :, c * 128 : (c + 1) * 128] += added[c]
        return carry

    lax.fori_loop(0, (NZ - 1) * 4, gather, 0)
    for a in range(AT):
        for side in range(2):
            at = a * TILE + side * 128
            wide[side, pl.ds(a, 32, stride=AT), :] = own[:, :, at : at + 128].reshape(32, 128)
    for side in range(2):
        rows = wide[side, pl.ds(0, 32 * AT), :].reshape(32, AT, 128)
        out_ref[:, :, side * 128 : (side + 1) * 128] = rows.astype(jnp.bfloat16)

    for copy in pending:
        copy.wait_send()
    for step in range(STEPS):
        def drain(g, carry, step=step):
            zd, q = group_of(step, g, y)

            @pl.when(zd != z)
            def _():
                row_copy(step, g, zd, q).wait_send()

            return carry

        lax.fori_loop(0, GROUPS, drain, 0)


def shards(amps, ints, task_cd, task_ab, task_count):
    smem = pl.BlockSpec(memory_space=pltpu.SMEM)
    vmem = pl.BlockSpec(memory_space=pltpu.VMEM)
    dma = pltpu.SemaphoreType.DMA
    return pl.pallas_call(
        kernel,
        out_shape=jax.ShapeDtypeStruct((32, AT, TILE), jnp.bfloat16),
        in_specs=[vmem, pl.BlockSpec(memory_space=pl.ANY), smem, smem, smem],
        out_specs=vmem,
        scratch_shapes=[
            pltpu.VMEM((KT * AT + 1, TILE, TILE), jnp.bfloat16),
            pltpu.VMEM((2, 128 * KT, 128), jnp.float32),
            pltpu.VMEM((8, 128), jnp.int32),
            pltpu.SMEM((8, 128), jnp.int32),
            pltpu.VMEM((STEPS, 32 * GROUPS, KT * TILE), jnp.bfloat16),
            pltpu.VMEM((STEPS, 32 * GROUPS, WIDE), jnp.float32),
            pltpu.VMEM((STEPS, 2, HALF_MSG, 16, 128), jnp.int16),
            pltpu.VMEM((STEPS, 2, HALF_MSG, 16, 128), jnp.int16),
            pltpu.VMEM((STEPS, 2, FULL_MSG, 16, 128), jnp.int16),
            pltpu.VMEM((STEPS, 2, FULL_MSG, 16, 128), jnp.int16),
            pltpu.VMEM((STEPS, GROUPS, ROW_MSG, 16, 128), jnp.int16),
            pltpu.VMEM((NZ, 4, ROW_MSG, 16, 128), jnp.int16),
            pltpu.VMEM((4, 8, WIDE), jnp.float32),
            dma, dma, dma((4, 4)), dma((3, 4)), dma((STEPS, GROUPS)),
            dma((STEPS, 2)), dma((STEPS, 2)), dma((STEPS, 2)), dma((STEPS, 2)),
            dma((STEPS, GROUPS)), dma((NZ, 4)),
        ],
        compiler_params=pltpu.CompilerParams(
            collective_id=0, has_side_effects=True, vmem_limit_bytes=60 * 1024 * 1024
        ),
    )(amps, ints, task_cd, task_ab, task_count)


def solution(mesh):
    in_specs = (P("row", "col", None), P(("row", "col"), None, None)) + (P(("row", "col")),) * 3
    return jax.shard_map(
        shards, mesh=mesh, in_specs=in_specs, out_specs=P("col", "row", None), check_vma=False
    )
```

time: 193 us -> 91.4 us (0.47)
  waiting for transfers between devices: 136 us -> 0 us
  Pallas kernels: 0 us -> 89 us
  local copies, waits for them, and re-layouts: 25.3 us -> 1.57 us
  matrix products: 14.5 us -> 0 us
  between operations: 13.8 us -> 0.66 us
  other arithmetic: 2.57 us -> 0 us
    reduce_scatter x2 -> x0, waiting for transfers between devices: 121 us -> none  [sum_by_axis(): value = lax.psum_scatter(value, axis, scatter_dimension=dim, tiled=True)]
    pallas_call x0 -> x1, Pallas kernels: none -> 89 us  [shards(): pl.pallas_call(kernel, out_shape=jax.ShapeDtypeStruct((32, AT, TILE), jnp...]
    gather x2 -> x0, local copies, waits for them, and re-layouts: 20.5 us -> none  [dense_tiles(): jnp.take(ints, found, axis=0)]
    dot_general x1 -> x0, matrix products: 14.5 us -> none  [ladder_term(): jnp.einsum('nkt,aktu->nau', rows_amps, table, preferred_element_type=jnp....]
    all_gather x1 -> x0, waiting for transfers between devices: 14.4 us -> none  [shards(): whole = lax.all_gather(amps, 'row', axis=0, tiled=True)]
    reduce_scatter x1 -> x0, local copies, waits for them, and re-layouts: 2.66 us -> none  [sum_by_axis(): value = lax.psum_scatter(value, axis, scatter_dimension=dim, tiled=True)]
  transfers between devices with their start and end apart: 3 -> 0, of which waited for: 3 -> 0; matrix products, arithmetic and copies ran while one was open for 11% -> 0% of each run, Pallas kernels for 0% -> 0%
where the time goes in v1:
time: 91.4 us; the launch traced here: 91.3 us
  Pallas kernels  89 us (97%)
  local copies, waits for them, and re-layouts  1.57 us (2%)
    pallas_call x1, Pallas kernels, shards(): pl.pallas_call(kernel, out_shape=jax.ShapeDtypeStruct((32, AT, TILE), jnp...  89 us

profile of v1, /device:TPU:16, one launch (start us, length us, event | category | flops | bytes accessed | tf_op | source)
XLA Modules:
  0.0 91.3 jit_solution(17364787053328213560)
XLA Ops:
  0.7 89.0 %shard_map.55 = bf16[32,8,256]{2,1,0:T(8,128)(2,1)} custom-call(bf16[128,8,256]{2,1,0:T(8,128)(2,1)} %amps_ref.1, bf16[64,256,256]{2,1,0:T(8,128)(2,1)} %ints_ref.1, s32[64]{0:T(128)} %cd_ref.1, s32[64]{0:T(128)} %ab_ref.1, s32[1]{0:T(128)S(6)} %copy.7.count_ref), custom_call_target="tpu_custom_call" | custom-call | tf_op jit(solution)/shard_map/pallas_call | solution.py:345
  89.7 1.6 %copy.8 = bf16[32,8,256]{2,1,0:T(8,128)(2,1)} copy(bf16[32,8,256]{2,1,0:T(8,128)(2,1)} %shard_map.55) | data formatting | bytes 262144

commit v2 on v0

v2 whole, which is shorter than its diff:
```python
import functools

import jax
import jax.numpy as jnp
from jax import lax
from jax.experimental import pallas as pl
from jax.experimental.pallas import tpu as pltpu
from jax.sharding import PartitionSpec as P

MESH = pl.DeviceIdType.MESH
NX, NY, NZ = 4, 4, 8
TILE = 256
KT = 8
AT = 8
WIDE = AT * TILE
LANES = WIDE // 128
HALF = LANES // 2
STEPS, UNITS = 4, 4
LOADS = 4
TOP = 32000.0
OCTAVE = 16.0
HALF_MSG = 2 * HALF + 1
ROW_MSG = 2 * LANES + 1


def place(delta, core, h):
    if delta == 0:
        return 0, core * 2 + h
    if delta == 2:
        return 2 + h, 2 + core
    if h == 0:
        return 1, core + (0 if delta == 1 else 2)
    return (2 if delta == 1 else 3), core


def unit_of(step, u, y):
    if step == 0:
        return 2 * y + u // 2, u % 2
    first, core = u < 2, u % 2
    if step == 1:
        delta, h = jnp.where(first, 1, 3), 0
    elif step == 2:
        delta, h = jnp.where(first, 1, 2), jnp.where(first, 1, 0)
    else:
        delta, h = jnp.where(first, 3, 2), 1
    return 2 * lax.rem(y + delta, NY) + core, h


def kernel(
    amps_ref, ints_ref, cd_ref, ab_ref, count_ref, out_ref,
    tiles, wide, table_v, table_s, lhs, part, hs, hr, fs, fr, zs, cr, zr,
    ints_sem, table_sem, block_sent, rows_sent, h_sent, f_sent, z_sent,
    ag_recv, h_recv, f_recv, c_recv, z_recv,
):
    row, col = lax.axis_index("row"), lax.axis_index("col")
    y, core = row // 2, row % 2
    z, x = col // NX, col % NX
    partner = (2 * y + 1 - core, col)
    y_up = (2 * lax.rem(y + 1, NY) + core, col)
    y_down = (2 * lax.rem(y + NY - 1, NY) + core, col)
    x_right, x_left, x_across = lax.rem(x + 1, NX), lax.rem(x + NX - 1, NX), lax.rem(x + 2, NX)
    right, left = (row, z * NX + x_right), (row, z * NX + x_left)
    lane = lax.broadcasted_iota(jnp.int32, (8, 128), 1)

    barrier = pltpu.get_barrier_semaphore()
    for peer in (partner, y_up, y_down, right, left):
        pl.semaphore_signal(barrier, inc=1, device_id=peer, device_id_type=MESH)
    for dz in (1, 2, NZ - 2, NZ - 1):
        peer = (row, lax.rem(z + dz, NZ) * NX + x)
        pl.semaphore_signal(barrier, inc=1, device_id=peer, device_id_type=MESH)

    loads = []
    for n in range(LOADS):
        some = pl.ds(n * (KT * AT // LOADS), KT * AT // LOADS)
        loads.append(pltpu.make_async_copy(ints_ref.at[some], tiles.at[some], ints_sem.at[n]))
        loads[-1].start()

    whole = amps_ref[...].astype(jnp.float32).reshape(128 * KT, TILE)
    for side in range(2):
        wide[side] = whole[:, side * 128 : (side + 1) * 128]
    for h in range(2):
        start = pl.multiple_of((core * 2 + h) * 64, 64)
        for k in range(KT):
            for side in range(2):
                rows = [wide[side, pl.ds((32 * xd + 16 * h) * KT + k, 16, stride=KT), :] for xd in range(NX)]
                at = k * TILE + side * 128
                lhs[0, pl.ds(start, 64), at : at + 128] = jnp.concatenate(rows, 0).astype(jnp.bfloat16)

    count = count_ref[0]

    def note(slot, table):
        key = jnp.where(slot < count, ab_ref[slot] * KT + cd_ref[slot], -1)
        return jnp.where(lane == key, slot, table)

    table_v[...] = lax.fori_loop(0, KT * AT, note, jnp.full((8, 128), KT * AT, jnp.int32))
    tiles[KT * AT] = jnp.zeros((TILE, TILE), jnp.bfloat16)
    move = pltpu.make_async_copy(table_v, table_s, table_sem)
    move.start()
    move.wait()
    pl.semaphore_wait(barrier, 9)

    def send(src, dst, send_sem, recv_sem, to):
        copy = pltpu.make_async_remote_copy(
            src_ref=src, dst_ref=dst, send_sem=send_sem, recv_sem=recv_sem, device_id=to, device_id_type=MESH
        )
        copy.start()

    def arrived(ref, sem):
        pltpu.make_async_remote_copy(
            src_ref=ref, dst_ref=ref, send_sem=block_sent, recv_sem=sem, device_id=partner, device_id_type=MESH
        ).wait_recv()

    def quarter(step, unit, e):
        return lhs.at[step, pl.ds(pl.multiple_of(unit * 64 + e * 32, 32), 32), :]

    def own_block(which):
        return lhs.at[0, pl.ds(pl.multiple_of(which * 128, 128), 128), :]

    def to_neighbours(h, e):
        mine = quarter(0, core * 2 + h, e)
        for delta, to in ((3, y_up), (1, y_down)):
            s, u = place(delta, core, h)
            send(mine, quarter(s, u, e), rows_sent, ag_recv.at[s, u, e], to)

    def pass_on(delta, h, e):
        s, u = place(delta, core, h)
        ref = quarter(s, u, e)
        arrived(ref, ag_recv.at[s, u, e])
        send(ref, ref, rows_sent, ag_recv.at[s, u, e], partner)
        if (delta, e) in ((1, 0), (3, 1)):
            s2, u2 = place(2, core, h)
            send(ref, quarter(s2, u2, e), rows_sent, ag_recv.at[s2, u2, e], y_down if delta == 1 else y_up)

    def from_partner(delta, h):
        s, u = place(delta, 1 - core, h)
        for e in range(2):
            arrived(quarter(s, u, e), ag_recv.at[s, u, e])

    send(own_block(core), own_block(core), block_sent, ag_recv.at[0, core, 0], partner)
    to_neighbours(0, 0)
    to_neighbours(0, 1)
    to_neighbours(1, 0)
    for copy in loads:
        copy.wait()

    def multiply(step, first=0, count=64 * UNITS, low=0, high=AT):
        rows = pl.ds(pl.multiple_of(first, 128), count)

        def one(a, carry):
            total = None
            for k in range(KT):
                term = jnp.dot(
                    lhs[step, rows, k * TILE : (k + 1) * TILE],
                    tiles[table_s[0, a * KT + k]],
                    preferred_element_type=jnp.float32,
                )
                total = term if total is None else total + term
            part[step, rows, pl.ds(pl.multiple_of(a * TILE, TILE), TILE)] = total
            return carry

        lax.fori_loop(low, high, one, 0)

    def encode(values, message):
        top = functools.reduce(jnp.maximum, [jnp.abs(v) for v in values])
        top = jnp.maximum(jnp.max(top, axis=1, keepdims=True), 1e-30)
        code = jnp.ceil(jnp.log2(top) * OCTAVE)
        factor = jnp.exp2(code * (-1.0 / OCTAVE)) * TOP
        for c, v in enumerate(values):
            message[c] = jnp.round(v * factor).astype(jnp.int32).astype(jnp.int16)
        message[len(values)] = jnp.broadcast_to(code, (8, 128)).astype(jnp.int32).astype(jnp.int16)

    def decode(message, n):
        def wide_of(c):
            return message[c].astype(jnp.int32).astype(jnp.float32)

        scale = jnp.exp2(wide_of(n) * (1.0 / OCTAVE)) * (1.0 / TOP)
        return [wide_of(c) * scale for c in range(n)]

    def rows_of(u, xd, i):
        return pl.ds(pl.multiple_of(u * 64 + xd * 16 + i * 8, 8), 8)

    def values_of(step, u, xd, first, last):
        return [part[step, rows_of(u, xd, i), c * 128 : (c + 1) * 128] for i in range(2) for c in range(first, last)]

    def add_into(step, u, xd, added):
        total = [v + w for v, w in zip(values_of(step, u, xd, 0, LANES), added)]
        for n, v in enumerate(total):
            part[step, rows_of(u, xd, n // LANES), n % LANES * 128 : (n % LANES + 1) * 128] = v
        return total

    def half_copy(step, u, way):
        return pltpu.make_async_remote_copy(
            src_ref=hs.at[step, u, way], dst_ref=hr.at[step, u, way], send_sem=h_sent,
            recv_sem=h_recv.at[step, u, way], device_id=(right, left)[way], device_id_type=MESH,
        )

    def full_copy(step, u, way):
        return pltpu.make_async_remote_copy(
            src_ref=fs.at[step, u, way], dst_ref=fr.at[step, u, way], send_sem=f_sent,
            recv_sem=f_recv.at[step, u, way], device_id=(right, left)[way], device_id_type=MESH,
        )

    def offset(zd):
        return lax.rem(z - zd + NZ + NZ // 2, NZ) - NZ // 2

    def row_copy(step, u, zd, h):
        off = offset(zd)
        slot = jnp.where(off < 0, off + 2, off + 1)
        return pltpu.make_async_remote_copy(
            src_ref=zs.at[step * UNITS + u], dst_ref=zr.at[slot, h], send_sem=z_sent, recv_sem=z_recv.at[slot, h],
            device_id=(row, zd * NX + x), device_id_type=MESH,
        )

    def collect_copy(step, u, off):
        ahead = jnp.where(off == -4, 2, jnp.where(off == -3, 1, NZ - 1))
        slot = jnp.where(off == -4, 1, 0)
        return pltpu.make_async_remote_copy(
            src_ref=zs.at[step * UNITS + u], dst_ref=cr.at[step, u, slot], send_sem=z_sent,
            recv_sem=c_recv.at[step, u, slot], device_id=(row, lax.rem(z + ahead, NZ) * NX + x), device_id_type=MESH,
        )

    def stage_half(step, way, first=0, count=UNITS):
        def body(n, carry):
            u = first + n
            encode(values_of(step, u, x_across, way * HALF, (way + 1) * HALF), hs.at[step, u, way])
            half_copy(step, u, way).start()
            return carry

        lax.fori_loop(0, count, body, 0)

    def stage_full(step, way, first=0):
        def body(n, carry):
            u = lax.rem(first + n, UNITS)
            arrived(hr.at[step, u, way], h_recv.at[step, u, way])
            values = values_of(step, u, x_right if way == 0 else x_left, 0, LANES)
            for n, v in enumerate(decode(hr.at[step, u, way], 2 * HALF)):
                at = n // HALF * LANES + way * HALF + n % HALF
                values[at] = values[at] + v
            encode(values, fs.at[step, u, way])
            full_copy(step, u, way).start()
            return carry

        lax.fori_loop(0, UNITS, body, 0)

    def stage_rows(step, first=0):
        def body(n, carry):
            u = lax.rem(first + n, UNITS)
            zd, h = unit_of(step, u, y)
            off = offset(zd)
            for way in range(2):
                arrived(fr.at[step, u, way], f_recv.at[step, u, way])
            added = [v + w for v, w in zip(*[decode(fr.at[step, u, way], 2 * LANES) for way in range(2)])]
            encode(add_into(step, u, x, added), zs.at[step * UNITS + u])

            @pl.when((off == 1) | (off == -1))
            def _():
                row_copy(step, u, zd, h).start()

            @pl.when((off == 3) | (off < -2))
            def _():
                collect_copy(step, u, off).start()

            return carry

        lax.fori_loop(0, UNITS, body, 0)

    def stage_collect(step, first=0):
        def body(n, carry):
            u = lax.rem(first + n, UNITS)
            zd, h = unit_of(step, u, y)
            off = offset(zd)

            def take(slot):
                arrived(cr.at[step, u, slot], c_recv.at[step, u, slot])
                return decode(cr.at[step, u, slot], 2 * LANES)

            @pl.when(off == -2)
            def _():
                add_into(step, u, x, take(1))

            @pl.when((off == 2) | (off == -2))
            def _():
                encode(add_into(step, u, x, take(0)), zs.at[step * UNITS + u])
                row_copy(step, u, zd, h).start()

            return carry

        lax.fori_loop(0, UNITS, body, 0)

    multiply(0, core * 128, 128, 0, 4)
    stage_half(0, 0, core * 2, 2)
    multiply(0, core * 128, 128, 4, 8)
    stage_half(0, 1, core * 2, 2)
    arrived(own_block(1 - core), ag_recv.at[0, 1 - core, 0])
    multiply(0, 128 - core * 128, 128, 0, 4)
    stage_half(0, 0, 2 - core * 2, 2)
    multiply(0, 128 - core * 128, 128, 4, 8)
    stage_half(0, 1, 2 - core * 2, 2)
    pass_on(1, 0, 0)
    pass_on(3, 0, 0)
    pass_on(1, 0, 1)
    pass_on(3, 0, 1)
    to_neighbours(1, 1)
    stage_full(0, 0, core * 2)
    stage_full(0, 1, core * 2)

    pass_on(1, 1, 0)
    pass_on(3, 1, 0)
    from_partner(1, 0)
    from_partner(3, 0)
    multiply(1, low=0, high=4)
    stage_half(1, 0)
    multiply(1, low=4, high=8)
    stage_half(1, 1)
    pass_on(2, 0, 0)
    pass_on(2, 0, 1)
    stage_rows(0, core * 2)
    pass_on(1, 1, 1)
    pass_on(3, 1, 1)
    stage_full(1, 0)
    stage_full(1, 1)

    from_partner(1, 1)
    from_partner(2, 0)
    multiply(2, low=0, high=4)
    stage_half(2, 0)
    pass_on(2, 1, 0)
    pass_on(2, 1, 1)
    multiply(2, low=4, high=8)
    stage_half(2, 1)
    stage_collect(0, core * 2)

    from_partner(3, 1)
    from_partner(2, 1)
    multiply(3, low=0, high=4)
    stage_half(3, 0)
    stage_full(2, 0)
    multiply(3, low=4, high=8)
    stage_half(3, 1)
    stage_full(2, 1)
    stage_rows(1)
    stage_full(3, 0)
    stage_full(3, 1)
    stage_collect(1)
    stage_rows(2)
    stage_rows(3)
    stage_collect(2)
    stage_collect(3)

    up, mine_core = lax.rem(z // 2 - y + NY, NY), z % 2
    for h in range(2):
        places = [place(delta, mine_core, h) for delta in range(NY)]
        step, u = places[0]
        for delta in range(1, NY):
            step = jnp.where(up == delta, places[delta][0], step)
            u = jnp.where(up == delta, places[delta][1], u)
        total = values_of(step, u, x, 0, LANES)
        for source in range(4):
            arrived(zr.at[source, h], z_recv.at[source, h])
            total = [v + w for v, w in zip(total, decode(zr.at[source, h], 2 * LANES))]
        for n, v in enumerate(total):
            i, c = n // LANES, n % LANES
            wide[c % 2, pl.ds((h * 16 + i * 8) * AT + c // 2, 8, stride=AT), :] = v
    for side in range(2):
        rows = wide[side, pl.ds(0, 32 * AT), :].reshape(32, AT, 128)
        out_ref[:, :, side * 128 : (side + 1) * 128] = rows.astype(jnp.bfloat16)

    def all_sent(ref, sem):
        pltpu.make_async_remote_copy(
            src_ref=ref, dst_ref=ref, send_sem=sem, recv_sem=z_recv.at[0, 0], device_id=partner, device_id_type=MESH
        ).wait_send()

    all_sent(own_block(core), block_sent)
    all_sent(lhs.at[pl.ds(0, 3)], rows_sent)
    all_sent(hs, h_sent)
    all_sent(fs, f_sent)
    all_sent(zs.at[pl.ds(0, STEPS * UNITS - 2)], z_sent)


def shards(amps, ints, task_cd, task_ab, task_count):
    smem = pl.BlockSpec(memory_space=pltpu.SMEM)
    vmem = pl.BlockSpec(memory_space=pltpu.VMEM)
    dma = pltpu.SemaphoreType.DMA

    def message(*shape):
        return pltpu.VMEM((*shape, 8, 128), jnp.int16)

    return pl.pallas_call(
        kernel,
        out_shape=jax.ShapeDtypeStruct((32, AT, TILE), jnp.bfloat16),
        in_specs=[vmem, pl.BlockSpec(memory_space=pl.ANY), smem, smem, smem],
        out_specs=vmem,
        scratch_shapes=[
            pltpu.VMEM((KT * AT + 1, TILE, TILE), jnp.bfloat16),
            pltpu.VMEM((2, 128 * KT, 128), jnp.float32),
            pltpu.VMEM((8, 128), jnp.int32),
            pltpu.SMEM((8, 128), jnp.int32),
            pltpu.VMEM((STEPS, 64 * UNITS, KT * TILE), jnp.bfloat16),
            pltpu.VMEM((STEPS, 64 * UNITS, WIDE), jnp.float32),
            message(STEPS, UNITS, 2, HALF_MSG), message(STEPS, UNITS, 2, HALF_MSG),
            message(STEPS, UNITS, 2, ROW_MSG), message(STEPS, UNITS, 2, ROW_MSG),
            message(STEPS * UNITS, ROW_MSG), message(STEPS, UNITS, 2, ROW_MSG), message(4, 2, ROW_MSG),
            dma((LOADS,)), dma, dma, dma, dma, dma, dma,
            dma((STEPS, UNITS, 2)), dma((STEPS, UNITS, 2)), dma((STEPS, UNITS, 2)), dma((STEPS, UNITS, 2)), dma((4, 2)),
        ],
        compiler_params=pltpu.CompilerParams(
            collective_id=0, has_side_effects=True, vmem_limit_bytes=60 * 1024 * 1024
        ),
    )(amps, ints, task_cd, task_ab, task_count)


def solution(mesh):
    in_specs = (P("row", "col", None), P(("row", "col"), None, None)) + (P(("row", "col")),) * 3
    return jax.shard_map(
        shards, mesh=mesh, in_specs=in_specs, out_specs=P("col", "row", None), check_vma=False
    )
```

time: 193 us -> 69 us (0.36)
  the two profiles are of different devices: /device:TPU:16 before, /device:TPU:52 now
where the time goes in v2:
time: 69 us; the launch traced here: 68.9 us
  Pallas kernels  66.7 us (97%)
  local copies, waits for them, and re-layouts  1.57 us (2%)
    pallas_call x1, Pallas kernels, shards(): pl.pallas_call(kernel, out_shape=jax.ShapeDtypeStruct((32, AT, TILE), jnp...  66.7 us
    unnamed x1, local copies, waits for them, and re-layouts  1.57 us

profile of v2, /device:TPU:52, one launch (start us, length us, event | category | flops | bytes accessed | tf_op | source)
XLA Modules:
  0.0 68.9 jit_solution(14072676250485631850)
XLA Ops:
  0.7 66.7 %shard_map.55 = bf16[32,8,256]{2,1,0:T(8,128)(2,1)} custom-call(bf16[128,8,256]{2,1,0:T(8,128)(2,1)} %amps_ref.1, bf16[64,256,256]{2,1,0:T(8,128)(2,1)} %ints_ref.1, s32[64]{0:T(128)} %cd_ref.1, s32[64]{0:T(128)} %ab_ref.1, s32[1]{0:T(128)S(6)} %copy.7.count_ref), custom_call_target="tpu_custom_call" | custom-call | tf_op jit(solution)/shard_map/pallas_call | solution.py:388
  67.3 1.6 %copy.8 = bf16[32,8,256]{2,1,0:T(8,128)(2,1)} copy(bf16[32,8,256]{2,1,0:T(8,128)(2,1)} %shard_map.55) | data formatting | bytes 262144

commit v3 on v2

--- a/solution.py
+++ b/solution.py
@@ -47,9 +47,9 @@
 
 
 def kernel(
-    amps_ref, ints_ref, cd_ref, ab_ref, count_ref, out_ref,
-    tiles, wide, table_v, table_s, lhs, part, hs, hr, fs, fr, zs, cr, zr,
-    ints_sem, table_sem, block_sent, rows_sent, h_sent, f_sent, z_sent,
+    amps_hbm, ints_ref, cd_ref, ab_ref, count_ref, out_ref,
+    tiles, amps_ref, wide, table_v, table_s, lhs, part, hs, hr, fs, fr, zs, cr, zr,
+    amps_sem, ints_sem, table_sem, block_sent, rows_sent, h_sent, f_sent, z_sent,
     ag_recv, h_recv, f_recv, c_recv, z_recv,
 ):
     row, col = lax.axis_index("row"), lax.axis_index("col")
@@ -62,6 +62,8 @@
     right, left = (row, z * NX + x_right), (row, z * NX + x_left)
     lane = lax.broadcasted_iota(jnp.int32, (8, 128), 1)
 
+    bring = pltpu.make_async_copy(amps_hbm, amps_ref, amps_sem)
+    bring.start()
     barrier = pltpu.get_barrier_semaphore()
     for peer in (partner, y_up, y_down, right, left):
         pl.semaphore_signal(barrier, inc=1, device_id=peer, device_id_type=MESH)
@@ -75,6 +77,7 @@
         loads.append(pltpu.make_async_copy(ints_ref.at[some], tiles.at[some], ints_sem.at[n]))
         loads[-1].start()
 
+    bring.wait()
     whole = amps_ref[...].astype(jnp.float32).reshape(128 * KT, TILE)
     for side in range(2):
         wide[side] = whole[:, side * 128 : (side + 1) * 128]
@@ -212,7 +215,7 @@
         )
 
     def collect_copy(step, u, off):
-        ahead = jnp.where(off == -4, 2, jnp.where(off == -3, 1, NZ - 1))
+        ahead = jnp.where(off == -4, jnp.where(u % 2 == 0, 2, NZ - 2), jnp.where(off == -3, 1, NZ - 1))
         slot = jnp.where(off == -4, 1, 0)
         return pltpu.make_async_remote_copy(
             src_ref=zs.at[step * UNITS + u], dst_ref=cr.at[step, u, slot], send_sem=z_sent,
@@ -242,7 +245,7 @@
 
         lax.fori_loop(0, UNITS, body, 0)
 
-    def stage_rows(step, first=0):
+    def stage_rows(step, first=0, count=UNITS):
         def body(n, carry):
             u = lax.rem(first + n, UNITS)
             zd, h = unit_of(step, u, y)
@@ -262,7 +265,7 @@
 
             return carry
 
-        lax.fori_loop(0, UNITS, body, 0)
+        lax.fori_loop(0, count, body, 0)
 
     def stage_collect(step, first=0):
         def body(n, carry):
@@ -274,7 +277,7 @@
                 arrived(cr.at[step, u, slot], c_recv.at[step, u, slot])
                 return decode(cr.at[step, u, slot], 2 * LANES)
 
-            @pl.when(off == -2)
+            @pl.when(jnp.where(u % 2 == 0, off == -2, off == 2))
             def _():
                 add_into(step, u, x, take(1))
 
@@ -332,16 +335,16 @@
 
     from_partner(3, 1)
     from_partner(2, 1)
+    multiply(3, low=4, high=8)
+    stage_half(3, 1)
+    stage_full(2, 0)
+    stage_full(2, 1)
+    stage_rows(1)
     multiply(3, low=0, high=4)
     stage_half(3, 0)
-    stage_full(2, 0)
-    multiply(3, low=4, high=8)
-    stage_half(3, 1)
-    stage_full(2, 1)
-    stage_rows(1)
-    stage_full(3, 0)
     stage_full(3, 1)
     stage_collect(1)
+    stage_full(3, 0)
     stage_rows(2)
     stage_rows(3)
     stage_collect(2)
@@ -388,10 +391,11 @@
     return pl.pallas_call(
         kernel,
         out_shape=jax.ShapeDtypeStruct((32, AT, TILE), jnp.bfloat16),
-        in_specs=[vmem, pl.BlockSpec(memory_space=pl.ANY), smem, smem, smem],
+        in_specs=[pl.BlockSpec(memory_space=pl.ANY), pl.BlockSpec(memory_space=pl.ANY), smem, smem, smem],
         out_specs=vmem,
         scratch_shapes=[
             pltpu.VMEM((KT * AT + 1, TILE, TILE), jnp.bfloat16),
+            pltpu.VMEM((128, KT, TILE), jnp.bfloat16),
             pltpu.VMEM((2, 128 * KT, 128), jnp.float32),
             pltpu.VMEM((8, 128), jnp.int32),
             pltpu.SMEM((8, 128), jnp.int32),
@@ -400,7 +404,7 @@
             message(STEPS, UNITS, 2, HALF_MSG), message(STEPS, UNITS, 2, HALF_MSG),
             message(STEPS, UNITS, 2, ROW_MSG), message(STEPS, UNITS, 2, ROW_MSG),
             message(STEPS * UNITS, ROW_MSG), message(STEPS, UNITS, 2, ROW_MSG), message(4, 2, ROW_MSG),
-            dma((LOADS,)), dma, dma, dma, dma, dma, dma,
+            dma, dma((LOADS,)), dma, dma, dma, dma, dma, dma,
             dma((STEPS, UNITS, 2)), dma((STEPS, UNITS, 2)), dma((STEPS, UNITS, 2)), dma((STEPS, UNITS, 2)), dma((4, 2)),
         ],
         compiler_params=pltpu.CompilerParams(

time: 69 us -> 66.2 us (0.959)
  the two profiles are of different devices: /device:TPU:52 before, /device:TPU:16 now
where the time goes in v3:
time: 66.2 us; the launch traced here: 66.1 us
  Pallas kernels  63.9 us (97%)
  local copies, waits for them, and re-layouts  1.57 us (2%)
    pallas_call x1, Pallas kernels, shards(): pl.pallas_call(kernel, out_shape=jax.ShapeDtypeStruct((32, AT, TILE), jnp...  63.9 us
    unnamed x1, local copies, waits for them, and re-layouts  1.57 us

profile of v3, /device:TPU:16, one launch (start us, length us, event | category | flops | bytes accessed | tf_op | source)
XLA Modules:
  0.0 66.1 jit_solution(2918342907133449322)
XLA Ops:
  0.7 63.9 %shard_map.55 = bf16[32,8,256]{2,1,0:T(8,128)(2,1)} custom-call(bf16[128,8,256]{2,1,0:T(8,128)(2,1)} %amps_hbm.1, bf16[64,256,256]{2,1,0:T(8,128)(2,1)} %ints_ref.1, s32[64]{0:T(128)} %cd_ref.1, s32[64]{0:T(128)} %ab_ref.1, s32[1]{0:T(128)S(6)} %copy.7.count_ref), custom_call_target="tpu_custom_call" | custom-call | tf_op jit(solution)/shard_map/pallas_call | solution.py:391
  64.6 1.6 %copy.8 = bf16[32,8,256]{2,1,0:T(8,128)(2,1)} copy(bf16[32,8,256]{2,1,0:T(8,128)(2,1)} %shard_map.55) | data formatting | bytes 262144

commit v4 on v3

--- a/solution.py
+++ b/solution.py
@@ -89,17 +89,6 @@
                 at = k * TILE + side * 128
                 lhs[0, pl.ds(start, 64), at : at + 128] = jnp.concatenate(rows, 0).astype(jnp.bfloat16)
 
-    count = count_ref[0]
-
-    def note(slot, table):
-        key = jnp.where(slot < count, ab_ref[slot] * KT + cd_ref[slot], -1)
-        return jnp.where(lane == key, slot, table)
-
-    table_v[...] = lax.fori_loop(0, KT * AT, note, jnp.full((8, 128), KT * AT, jnp.int32))
-    tiles[KT * AT] = jnp.zeros((TILE, TILE), jnp.bfloat16)
-    move = pltpu.make_async_copy(table_v, table_s, table_sem)
-    move.start()
-    move.wait()
     pl.semaphore_wait(barrier, 9)
 
     def send(src, dst, send_sem, recv_sem, to):
@@ -143,6 +132,17 @@
     to_neighbours(0, 0)
     to_neighbours(0, 1)
     to_neighbours(1, 0)
+    count = count_ref[0]
+
+    def note(slot, table):
+        key = jnp.where(slot < count, ab_ref[slot] * KT + cd_ref[slot], -1)
+        return jnp.where(lane == key, slot, table)
+
+    table_v[...] = lax.fori_loop(0, KT * AT, note, jnp.full((8, 128), KT * AT, jnp.int32))
+    tiles[KT * AT] = jnp.zeros((TILE, TILE), jnp.bfloat16)
+    move = pltpu.make_async_copy(table_v, table_s, table_sem)
+    move.start()
+    move.wait()
     for copy in loads:
         copy.wait()
 

time: 66.2 us -> 66.4 us (level)
  no operation moved by 1% of the time
where the time goes in v4:
time: 66.4 us; the launch traced here: 66.3 us
  Pallas kernels  64.1 us (97%)
  local copies, waits for them, and re-layouts  1.57 us (2%)
    pallas_call x1, Pallas kernels, shards(): pl.pallas_call(kernel, out_shape=jax.ShapeDtypeStruct((32, AT, TILE), jnp...  64.1 us
    unnamed x1, local copies, waits for them, and re-layouts  1.57 us

profile of v4, /device:TPU:16, one launch (start us, length us, event | category | flops | bytes accessed | tf_op | source)
XLA Modules:
  0.0 66.3 jit_solution(4926038191080636876)
XLA Ops:
  0.7 64.1 %shard_map.55 = bf16[32,8,256]{2,1,0:T(8,128)(2,1)} custom-call(bf16[128,8,256]{2,1,0:T(8,128)(2,1)} %amps_hbm.1, bf16[64,256,256]{2,1,0:T(8,128)(2,1)} %ints_ref.1, s32[64]{0:T(128)} %cd_ref.1, s32[64]{0:T(128)} %ab_ref.1, s32[1]{0:T(128)S(6)} %copy.7.count_ref), custom_call_target="tpu_custom_call" | custom-call | tf_op jit(solution)/shard_map/pallas_call | solution.py:391
  64.8 1.6 %copy.8 = bf16[32,8,256]{2,1,0:T(8,128)(2,1)} copy(bf16[32,8,256]{2,1,0:T(8,128)(2,1)} %shard_map.55) | data formatting | bytes 262144
